TPU v7x, 32 devices: a whole 2x2x4 slice. The times are simulated.
32 devices in a mesh: cfg: 2 (over x), work: 16 (over z, y, core).
Axes of the slice: x: 2, y: 2, z: 4, core: 2. Of those that a mesh axis runs over, the one named last changes fastest.
Arguments:
- sources: bfloat16 [32, 16384, 128], P('cfg', 'work'), parts along dimension 0, may hold values from -6 to 6
- perambs: bfloat16 [192, 16384], P('cfg', 'work'), parts along dimension 0, may hold values from -0.5 to 0.5
- source_ids: int32 [16], replicated, may hold values from 0 to 15
- peramb_ids: int32 [48, 3], replicated, may hold values from 0 to 95
- sink_counts: int32 [16], replicated, may hold values from 1 to 6, 48 in all
- weights: float32 [48], replicated, may hold values from -2 to 2, as said below
Outputs:
- sink_tensors: bfloat16 [32, 16384, 128], P(('cfg', 'work')), parts along dimension 0
There are 2 independent parts, one for each index of `cfg`. A program takes and returns all parts, laid end to end along the dimension named above; an argument that names none is the same for every part. Nothing has to cross between parts.
Inputs may be any that keep to these rules, and one draw needn't show every extreme that they name: `sink_counts`: diagrams are listed sink by sink in order; the counts add up to 48 and some sink has exactly 6 diagrams. `weights`: nonzero multiples of 1/4.
All inputs are finite; a program needn't handle non-finite values.
Results may differ from a plain program's by a relative error of at most 0.0064.
Values may be sent and summed in bfloat16 or wider, within the bound.
A program may use at most 128 MiB of HBM per device.

v0:
```python
import functools

import jax
import jax.numpy as jnp
import numpy as np
from jax import lax
from jax.experimental import pallas as pl
from jax.experimental.pallas import tpu as pltpu
from jax.sharding import PartitionSpec as P

MOST = 6
LEGS = 3
CHUNKS = 4
PAD = 8
MESH = pl.DeviceIdType.MESH


def pick_kernel(ids_ref, x_ref, o_ref, buf, in_sem, out_sem):
    sinks = o_ref.shape[0]
    load = pltpu.make_async_copy(x_ref, buf, in_sem)
    load.start()
    load.wait()

    @pl.loop(0, sinks)
    def _(s):
        pltpu.make_async_copy(buf.at[ids_ref[s]], o_ref.at[s], out_sem.at[s]).start()

    @pl.loop(0, sinks)
    def _(s):
        pltpu.make_async_copy(buf.at[0], o_ref.at[s], out_sem.at[s]).wait()


def pick(sources, source_ids):
    sinks = source_ids.shape[0]
    shape = (sinks,) + sources.shape[1:]
    return pl.pallas_call(
        pick_kernel,
        out_shape=jax.ShapeDtypeStruct(shape, sources.dtype),
        in_specs=[
            pl.BlockSpec(memory_space=pltpu.SMEM),
            pl.BlockSpec(memory_space=pl.ANY),
        ],
        out_specs=pl.BlockSpec(memory_space=pl.ANY),
        scratch_shapes=[
            pltpu.VMEM(sources.shape, sources.dtype),
            pltpu.SemaphoreType.DMA,
            pltpu.SemaphoreType.DMA((sinks,)),
        ],
        compiler_params=pltpu.CompilerParams(vmem_limit_bytes=60 * 1024 * 1024),
        name="pick",
    )(source_ids, sources)


def contract_kernel(
    workers,
    parts,
    w_ref,
    key_ref,
    x_ref,
    legs_ref,
    o_ref,
    xbuf,
    lbuf,
    legs,
    p1s,
    p2s,
    p3s,
    mid,
    acc,
    obuf,
    own_sem,
    xsend,
    xrecv,
    lsend,
    lrecv,
    out_sem,
):
    per, extent = xbuf.shape[2], xbuf.shape[3]
    own_rows = lbuf.shape[2]
    count = workers * per
    step = extent + PAD
    me = lax.axis_index("work")

    def leg_copy(t):
        peer = lax.rem(me + t, workers)
        return pltpu.make_async_remote_copy(
            src_ref=legs_ref.at[peer],
            dst_ref=lbuf.at[me],
            send_sem=lsend.at[t],
            recv_sem=lrecv.at[t],
            device_id={"work": peer},
            device_id_type=MESH,
        )

    def x_copy(c, t):
        peer = lax.rem(me + t, workers)
        return pltpu.make_async_remote_copy(
            src_ref=x_ref.at[peer, pl.ds(c * per, per)],
            dst_ref=xbuf.at[c, me],
            send_sem=xsend.at[c, t],
            recv_sem=xrecv.at[c, t],
            device_id={"work": peer},
            device_id_type=MESH,
        )

    own = [pltpu.make_async_copy(legs_ref.at[me], lbuf.at[me], own_sem.at[parts])]
    for c in range(parts):
        own.append(
            pltpu.make_async_copy(
                x_ref.at[me, pl.ds(c * per, per)], xbuf.at[c, me], own_sem.at[c]
            )
        )
    for copy in own:
        copy.start()

    barrier = pltpu.get_barrier_semaphore()

    @pl.loop(1, workers)
    def _(t):
        peer = lax.rem(me + t, workers)
        pl.semaphore_signal(barrier, inc=1, device_id={"work": peer}, device_id_type=MESH)

    pl.semaphore_wait(barrier, workers - 1)

    @pl.loop(1, workers)
    def _(t):
        leg_copy(t).start()

    for c in range(parts):

        @pl.loop(1, workers)
        def _(t):
            x_copy(c, t).start()

    own[0].wait()

    @pl.loop(1, workers)
    def _(t):
        leg_copy(t).wait()

    @pl.loop(0, MOST * LEGS)
    def _(m):
        for v in range(workers):
            legs[m, v * own_rows : (v + 1) * own_rows, :] = lbuf[v, m].astype(jnp.float32)

    firsts = []
    for d in range(MOST):
        firsts.append(legs[LEGS * d].astype(jnp.bfloat16))
        p2s[d * extent : (d + 1) * extent, :] = legs[LEGS * d + 1].astype(jnp.bfloat16)
        p3s[d] = legs[LEGS * d + 2].T.astype(jnp.bfloat16)
    side = jnp.concatenate(firsts, axis=1)
    rows = lax.broadcasted_iota(jnp.int32, (MOST * extent, MOST * count), 0)
    for c in range(parts):
        chosen = jnp.where(rows == key_ref[c], 1.0, 0.0).astype(jnp.bfloat16)
        p1s[c] = jnp.dot(side, chosen, preferred_element_type=jnp.float32).astype(jnp.bfloat16)

    group = 4
    wide = 8
    for c in range(parts):
        own[c + 1].wait()

        @pl.loop(1, workers)
        def _(t):
            x_copy(c, t).wait()

        @pl.loop(0, count // group, unroll=2)
        def _(g):
            tiles = [xbuf[c, g * (group // per) + i // per, i % per] for i in range(group)]
            both = jnp.concatenate(tiles, axis=1)
            for d in range(MOST):
                z = jnp.dot(
                    p2s[d * extent : (d + 1) * extent, :], both, preferred_element_type=jnp.float32
                ).astype(jnp.bfloat16)
                stacked = jnp.concatenate(
                    [z[:, i * extent : (i + 1) * extent] for i in range(group)], axis=0
                )
                y = jnp.dot(stacked, p3s[d], preferred_element_type=jnp.float32) * w_ref[d]
                for i in range(group):
                    at = pl.multiple_of((d * count + group * g + i) * step, 8)
                    mid[pl.ds(at, extent), :] = y[i * extent : (i + 1) * extent]

        @pl.loop(0, extent // wide)
        def _(b):
            cols = [
                mid[pl.ds(wide * b + h, MOST * count, stride=step), :].astype(jnp.bfloat16)
                for h in range(wide)
            ]
            t = jnp.dot(
                p1s[c], jnp.concatenate(cols, axis=1), preferred_element_type=jnp.float32
            )
            for h in range(wide):
                at = pl.ds(pl.multiple_of((wide * b + h) * step, 8), extent)
                piece = t[:, h * extent : (h + 1) * extent]
                if c > 0:
                    piece = piece + acc[at, :]
                acc[at, :] = piece

    span = 16
    for g in range(extent // span):

        @pl.loop(0, span, unroll=4)
        def _(i):
            a = g * span + i
            obuf[a] = acc[pl.ds(a, extent, stride=step), :].astype(jnp.bfloat16)

        pltpu.make_async_copy(
            obuf.at[pl.ds(g * span, span)], o_ref.at[pl.ds(g * span, span)], out_sem.at[g]
        ).start()
    for g in range(extent // span):
        pltpu.make_async_copy(
            obuf.at[pl.ds(g * span, span)], o_ref.at[pl.ds(g * span, span)], out_sem.at[g]
        ).wait()


def contract(x, legs, w, workers):
    own_a, extent = x.shape[1], x.shape[2]
    parts = min(CHUNKS, own_a)
    per = own_a // parts
    count = workers * per
    col = np.arange(MOST * count)
    keys = [
        col // count * extent + col % count // per * own_a + c * per + col % per
        for c in range(parts)
    ]
    key = jnp.asarray(np.stack(keys)[:, None, :], jnp.int32)
    step = extent + PAD
    return pl.pallas_call(
        functools.partial(contract_kernel, workers, parts),
        out_shape=jax.ShapeDtypeStruct((extent, extent, extent), jnp.bfloat16),
        in_specs=[
            pl.BlockSpec(memory_space=pltpu.SMEM),
            pl.BlockSpec(memory_space=pltpu.VMEM),
            pl.BlockSpec(memory_space=pl.ANY),
            pl.BlockSpec(memory_space=pl.ANY),
        ],
        out_specs=pl.BlockSpec(memory_space=pl.ANY),
        scratch_shapes=[
            pltpu.VMEM((parts, workers, per, extent, extent), jnp.bfloat16),
            pltpu.VMEM((workers,) + legs.shape[1:], jnp.bfloat16),
            pltpu.VMEM((MOST * LEGS, extent, extent), jnp.float32),
            pltpu.VMEM((parts, extent, MOST * count), jnp.bfloat16),
            pltpu.VMEM((MOST * extent, extent), jnp.bfloat16),
            pltpu.VMEM((MOST, extent, extent), jnp.bfloat16),
            pltpu.VMEM((MOST * count * step, extent), jnp.float32),
            pltpu.VMEM((extent * step, extent), jnp.float32),
            pltpu.VMEM((extent, extent, extent), jnp.bfloat16),
            pltpu.SemaphoreType.DMA((parts + 1,)),
            pltpu.SemaphoreType.DMA((parts, workers)),
            pltpu.SemaphoreType.DMA((parts, workers)),
            pltpu.SemaphoreType.DMA((workers,)),
            pltpu.SemaphoreType.DMA((workers,)),
            pltpu.SemaphoreType.DMA((extent // 16,)),
        ],
        compiler_params=pltpu.CompilerParams(
            vmem_limit_bytes=62 * 1024 * 1024, collective_id=0, has_side_effects=True
        ),
        name="contract",
    )(w, key, x, legs)


def per_device(sources, perambs, source_ids, peramb_ids, sink_counts, weights):
    workers = lax.axis_size("work")
    extent = sources.shape[2]
    own_a = sources.shape[1] // extent
    diagrams = peramb_ids.shape[0]

    picked = pick(sources.reshape(-1, own_a, extent, extent), source_ids)
    starts = jnp.cumsum(sink_counts) - sink_counts
    slots = jnp.arange(MOST, dtype=jnp.int32)
    chosen = jnp.minimum(starts[:, None] + slots[None, :], diagrams - 1)
    ids = peramb_ids[chosen].reshape(-1)
    onehot = (ids[:, None] == jnp.arange(perambs.shape[0], dtype=jnp.int32)[None, :]).astype(
        jnp.bfloat16
    )
    legs = jnp.dot(onehot, perambs, preferred_element_type=jnp.bfloat16)
    legs = legs.reshape(workers, MOST * LEGS, -1, extent)
    own = lax.axis_index("work")
    own_ids = lax.dynamic_index_in_dim(chosen, own, 0, keepdims=False)
    own_count = lax.dynamic_index_in_dim(sink_counts, own, 0, keepdims=False)
    w = jnp.where(slots < own_count, weights[own_ids], 0.0)
    total = contract(picked, legs, w, workers)
    return total.reshape(1, extent * extent, extent)


def solution(mesh):
    return jax.shard_map(
        per_device,
        mesh=mesh,
        in_specs=(P("cfg", "work", None), P("cfg", "work"), P(), P(), P(), P()),
        out_specs=P(("cfg", "work"), None, None),
        check_vma=False,
    )
```

profile of v0, /device:TPU:29, one launch (start us, length us, event | category | flops | bytes accessed | tf_op | source)
XLA Modules:
  0.0 139.5 jit_solution(3958310820176376549)
XLA Ops:
  0.0 0.0 copy-start
  0.0 1.4 dynamic_slice.8
  1.4 0.7 copy.10
  2.1 0.1 reduce
  2.2 0.7 sub.3
  2.9 0.6 dynamic-slice
  3.5 0.7 fusion.1
  4.2 1.3 gather_fusion
  5.5 1.3 compare_select_fusion.2.w_ref
  6.7 0.1 compare_select_fusion
  6.8 0.1 reshape.121
  6.9 0.8 copy.11
  7.7 0.6 gather_fusion.1
  8.3 0.2 eq.15
  8.5 0.0 copy-done
  8.5 0.4 convolution_bitcast_fusion
  8.8 0.9 copy.12
  9.8 5.0 %pick.1.x_ref = bf16[16,8,128,128]{3,2,1,0:T(8,128)(2,1)} custom-call(s32[16]{0:T(128)} %ids_ref.1, bf16[16,8,128,128]{3,2,1,0:T(8,128)(2,1)} %bitcast.18), custom_call_target="tpu_custom_call" | custom-call | tf_op jit(solution)/shard_map/pick/pallas_call | solution.py:36
  14.8 121.0 %contract.1 = bf16[128,128,128]{2,1,0:T(8,128)(2,1)} custom-call(f32[6]{0:T(128)} %compare_select_fusion.2.w_ref, s32[4,1,192]{2,1,0:T(1,128)} %constant.28.clone.key_ref, bf16[16,8,128,128]{3,2,1,0:T(8,128)(2,1)} %pick.1.x_ref, bf16[16,18,8,128]{3,2,1,0:T(8,128)(2,1)} %bitcast.19), custom_call_target="tpu_custom_call" | custom-call | tf_op jit(solution)/shard_map/contract/pallas_call | solution.py:227
  135.8 3.7 %copy.14 = bf16[1,16384,128]{2,1,0:T(8,128)(2,1)} copy(bf16[1,16384,128]{2,1,0:T(8,128)(2,1)} %bitcast.17) | data formatting | bytes 8388608
  (3 shorter events, 0.0 us)
Async XLA Ops:
  0.0 8.5 %copy-start = (bf16[96,1024]{1,0:T(8,128)(2,1)S(1)}, bf16[96,1024]{1,0:T(8,128)(2,1)}, u32[]{:S(2)}) copy-start(bf16[96,1024]{1,0:T(8,128)(2,1)} %param.8) | copy-start | bytes 589828
where the time goes:
time: 140 us
  Pallas kernels  126 us (90%)
  local copies, waits for them, and re-layouts  10.3 us (7%)
  other arithmetic  2.81 us (2%)
    pallas_call x1, Pallas kernels, contract(): pl.pallas_call(functools.partial(contract_kernel, workers, parts), out_sh...  121 us
    unnamed x5, local copies, waits for them, and re-layouts  5.44 us
    pallas_call x1, Pallas kernels, pick(): pl.pallas_call(pick_kernel, out_shape=jax.ShapeDtypeStruct(shape, sources...  4.99 us

commit v1 on v0

v1 whole, which is shorter than its diff:
```python
import functools

import jax
import jax.numpy as jnp
import numpy as np
from jax import lax
from jax.experimental import pallas as pl
from jax.experimental.pallas import tpu as pltpu
from jax.sharding import PartitionSpec as P

MOST = 6
LEGS = 3
PAD = 8
MESH = pl.DeviceIdType.MESH


def pick_kernel(
    ids_ref, legs_ids_ref, counts_ref, x_ref, p_ref, o_ref, l_ref, buf, rows, in_sem, out_sem
):
    sinks = o_ref.shape[0]
    diagrams = legs_ids_ref.shape[0] // LEGS
    own_rows, extent = l_ref.shape[2], l_ref.shape[3]
    load = pltpu.make_async_copy(x_ref, buf, in_sem)
    load.start()

    for r in range(own_rows):
        rows[:, r, :] = p_ref[:, r * extent : (r + 1) * extent].astype(jnp.float32)

    load.wait()

    @pl.loop(0, sinks)
    def _(s):
        pltpu.make_async_copy(buf.at[ids_ref[s]], o_ref.at[s], out_sem.at[s]).start()

    def one(s, start):
        for slot in range(MOST):
            d = jnp.minimum(start + slot, diagrams - 1)
            for leg in range(LEGS):
                l_ref[s, slot * LEGS + leg] = rows[legs_ids_ref[d * LEGS + leg]].astype(
                    jnp.bfloat16
                )
        return start + counts_ref[s]

    lax.fori_loop(0, sinks, one, jnp.int32(0))

    @pl.loop(0, sinks)
    def _(s):
        pltpu.make_async_copy(buf.at[0], o_ref.at[s], out_sem.at[s]).wait()


def pick(sources, perambs, source_ids, leg_ids, counts):
    sinks = source_ids.shape[0]
    own_rows, extent = sources.shape[1], sources.shape[3]
    smem = pl.BlockSpec(memory_space=pltpu.SMEM)
    return pl.pallas_call(
        pick_kernel,
        out_shape=(
            jax.ShapeDtypeStruct((sinks,) + sources.shape[1:], sources.dtype),
            jax.ShapeDtypeStruct((sinks, MOST * LEGS, own_rows, extent), perambs.dtype),
        ),
        in_specs=[
            smem,
            smem,
            smem,
            pl.BlockSpec(memory_space=pl.ANY),
            pl.BlockSpec(memory_space=pltpu.VMEM),
        ],
        out_specs=(
            pl.BlockSpec(memory_space=pl.ANY),
            pl.BlockSpec(memory_space=pltpu.VMEM),
        ),
        scratch_shapes=[
            pltpu.VMEM(sources.shape, sources.dtype),
            pltpu.VMEM((perambs.shape[0], own_rows, extent), jnp.float32),
            pltpu.SemaphoreType.DMA,
            pltpu.SemaphoreType.DMA((sinks,)),
        ],
        compiler_params=pltpu.CompilerParams(vmem_limit_bytes=60 * 1024 * 1024),
        name="pick",
    )(source_ids, leg_ids, counts, sources, perambs)


def split_rows(own_a):
    sizes, left = [], own_a
    while left > 0:
        sizes.append(2 if left > 2 else 1)
        left -= sizes[-1]
    return sizes


def contract_kernel(
    workers,
    counts_ref,
    weights_ref,
    key_ref,
    x_ref,
    legs_ref,
    o_ref,
    xbuf,
    lbuf,
    legs,
    p1s,
    p2s,
    p3s,
    mid,
    acc,
    stage,
    obuf,
    own_sem,
    xsend,
    xrecv,
    lsend,
    lrecv,
    out_sem,
):
    own_a, extent = xbuf.shape[0], xbuf.shape[2]
    diagrams = weights_ref.shape[0]
    sizes = split_rows(own_a)
    step = extent + PAD
    me = lax.axis_index("work")

    def leg_copy(t):
        peer = lax.rem(me + t, workers)
        return pltpu.make_async_remote_copy(
            src_ref=legs_ref.at[peer],
            dst_ref=lbuf.at[me],
            send_sem=lsend.at[t],
            recv_sem=lrecv.at[t],
            device_id={"work": peer},
            device_id_type=MESH,
        )

    def x_copy(j, t):
        peer = lax.rem(me + t, workers)
        return pltpu.make_async_remote_copy(
            src_ref=x_ref.at[peer, j],
            dst_ref=xbuf.at[j, me],
            send_sem=xsend.at[j, t],
            recv_sem=xrecv.at[j, t],
            device_id={"work": peer},
            device_id_type=MESH,
        )

    own = [
        pltpu.make_async_copy(x_ref.at[me, j], xbuf.at[j, me], own_sem.at[j])
        for j in range(own_a)
    ]
    own.append(pltpu.make_async_copy(legs_ref.at[me], lbuf.at[me], own_sem.at[own_a]))
    for copy in own:
        copy.start()

    barrier = pltpu.get_barrier_semaphore()

    @pl.loop(1, workers)
    def _(t):
        peer = lax.rem(me + t, workers)
        pl.semaphore_signal(barrier, inc=1, device_id={"work": peer}, device_id_type=MESH)

    pl.semaphore_wait(barrier, workers - 1)

    @pl.loop(1, workers)
    def _(t):
        leg_copy(t).start()

    @pl.loop(0, own_a)
    def _(j):
        @pl.loop(1, workers)
        def _(t):
            x_copy(j, t).start()

    start = lax.fori_loop(
        0, workers, lambda s, v: v + jnp.where(s < me, counts_ref[s], 0), jnp.int32(0)
    )
    factors = []
    for d in range(MOST):
        value = weights_ref[jnp.minimum(start + d, diagrams - 1)]
        factors.append(jnp.where(d < counts_ref[me], value, 0.0))

    own[own_a].wait()

    @pl.loop(1, workers)
    def _(t):
        leg_copy(t).wait()

    own_rows = lbuf.shape[2]

    @pl.loop(0, MOST * LEGS)
    def _(m):
        for v in range(workers):
            legs[m, v * own_rows : (v + 1) * own_rows, :] = lbuf[v, m].astype(jnp.float32)

    firsts = []
    for d in range(MOST):
        firsts.append(legs[LEGS * d].astype(jnp.bfloat16))
        p2s[d * extent : (d + 1) * extent, :] = legs[LEGS * d + 1].astype(jnp.bfloat16)
        p3s[d] = legs[LEGS * d + 2].T.astype(jnp.bfloat16)
    side = jnp.concatenate(firsts, axis=1)
    low = 0
    for c, size in enumerate(sizes):
        width = MOST * size * workers
        rows = lax.broadcasted_iota(jnp.int32, (MOST * extent, width), 0)
        chosen = jnp.where(rows == key_ref[c, :, :width], 1.0, 0.0).astype(jnp.bfloat16)
        p1s[c, :, :width] = jnp.dot(side, chosen, preferred_element_type=jnp.float32).astype(
            jnp.bfloat16
        )

    group = 4
    wide = 8
    for c, size in enumerate(sizes):
        count = size * workers
        for j in range(low, low + size):
            own[j].wait()

            @pl.loop(1, workers)
            def _(t):
                x_copy(j, t).wait()

        @pl.loop(0, count // group, unroll=2)
        def _(g):
            j = low + lax.div(g * group, workers)
            v = lax.rem(g * group, workers)
            both = jnp.concatenate([xbuf[j, v + i] for i in range(group)], axis=1)
            for d in range(MOST):
                z = jnp.dot(
                    p2s[d * extent : (d + 1) * extent, :], both, preferred_element_type=jnp.float32
                ).astype(jnp.bfloat16)
                stacked = jnp.concatenate(
                    [z[:, i * extent : (i + 1) * extent] for i in range(group)], axis=0
                )
                y = jnp.dot(stacked, p3s[d], preferred_element_type=jnp.float32) * factors[d]
                for i in range(group):
                    at = pl.multiple_of((d * count + group * g + i) * step, 8)
                    mid[pl.ds(at, extent), :] = y[i * extent : (i + 1) * extent]

        low += size

        def pieces(b):
            cols = [
                mid[pl.ds(wide * b + h, MOST * count, stride=step), :].astype(jnp.bfloat16)
                for h in range(wide)
            ]
            t = jnp.dot(
                p1s[c, :, : MOST * count],
                jnp.concatenate(cols, axis=1),
                preferred_element_type=jnp.float32,
            )
            out = []
            for h in range(wide):
                at = pl.ds(pl.multiple_of((wide * b + h) * extent, 8), extent)
                piece = t[:, h * extent : (h + 1) * extent]
                out.append((at, piece if c == 0 else piece + acc[at, :]))
            return out

        if c < len(sizes) - 1:

            @pl.loop(0, extent // wide)
            def _(b):
                for at, piece in pieces(b):
                    acc[at, :] = piece

        else:

            @pl.loop(0, extent // (2 * wide))
            def _(b):
                for half in range(2):
                    for h, (at, piece) in enumerate(pieces(2 * b + half)):
                        stage[:, half * wide + h, :] = piece
                at = pl.ds(pl.multiple_of(2 * wide * b, 2 * wide), 2 * wide)
                obuf[:, at, :] = stage[:, : 2 * wide, :].astype(jnp.bfloat16)
                pltpu.make_async_copy(obuf.at[:, at], o_ref.at[:, at], out_sem.at[b]).start()

            @pl.loop(0, extent // (2 * wide))
            def _(b):
                at = pl.ds(pl.multiple_of(2 * wide * b, 2 * wide), 2 * wide)
                pltpu.make_async_copy(obuf.at[:, at], o_ref.at[:, at], out_sem.at[b]).wait()


def contract(x, legs, counts, weights, workers):
    own_a, extent = x.shape[1], x.shape[2]
    sizes = split_rows(own_a)
    most = max(sizes) * workers
    keys = np.full((len(sizes), 1, MOST * most), -1)
    low = 0
    for c, size in enumerate(sizes):
        count = size * workers
        col = np.arange(MOST * count)
        at = col % count
        keys[c, 0, : MOST * count] = (
            col // count * extent + at % workers * own_a + low + at // workers
        )
        low += size
    step = extent + PAD
    smem = pl.BlockSpec(memory_space=pltpu.SMEM)
    return pl.pallas_call(
        functools.partial(contract_kernel, workers),
        out_shape=jax.ShapeDtypeStruct((extent, extent, extent), jnp.bfloat16),
        in_specs=[
            smem,
            smem,
            pl.BlockSpec(memory_space=pltpu.VMEM),
            pl.BlockSpec(memory_space=pl.ANY),
            pl.BlockSpec(memory_space=pl.ANY),
        ],
        out_specs=pl.BlockSpec(memory_space=pl.ANY),
        scratch_shapes=[
            pltpu.VMEM((own_a, workers, extent, extent), jnp.bfloat16),
            pltpu.VMEM((workers,) + legs.shape[1:], jnp.bfloat16),
            pltpu.VMEM((MOST * LEGS, extent, extent), jnp.float32),
            pltpu.VMEM((len(sizes), extent, MOST * most), jnp.bfloat16),
            pltpu.VMEM((MOST * extent, extent), jnp.bfloat16),
            pltpu.VMEM((MOST, extent, extent), jnp.bfloat16),
            pltpu.VMEM((MOST * most * step, extent), jnp.float32),
            pltpu.VMEM((extent * extent, extent), jnp.float32),
            pltpu.VMEM((extent, 24, extent), jnp.float32),
            pltpu.VMEM((extent, extent, extent), jnp.bfloat16),
            pltpu.SemaphoreType.DMA((own_a + 1,)),
            pltpu.SemaphoreType.DMA((own_a, workers)),
            pltpu.SemaphoreType.DMA((own_a, workers)),
            pltpu.SemaphoreType.DMA((workers,)),
            pltpu.SemaphoreType.DMA((workers,)),
            pltpu.SemaphoreType.DMA((extent // 16,)),
        ],
        compiler_params=pltpu.CompilerParams(
            vmem_limit_bytes=62 * 1024 * 1024, collective_id=0, has_side_effects=True
        ),
        name="contract",
    )(counts, weights, jnp.asarray(keys, jnp.int32), x, legs)


def per_device(sources, perambs, source_ids, peramb_ids, sink_counts, weights):
    workers = lax.axis_size("work")
    extent = sources.shape[2]
    own_a = sources.shape[1] // extent
    picked, legs = pick(
        sources.reshape(-1, own_a, extent, extent),
        perambs,
        source_ids,
        peramb_ids.reshape(-1),
        sink_counts,
    )
    total = contract(picked, legs, sink_counts, weights, workers)
    return total.reshape(1, extent * extent, extent)


def solution(mesh):
    return jax.shard_map(
        per_device,
        mesh=mesh,
        in_specs=(P("cfg", "work", None), P("cfg", "work"), P(), P(), P(), P()),
        out_specs=P(("cfg", "work"), None, None),
        check_vma=False,
    )
```

time: 140 us -> 137 us (0.979)
  local copies, waits for them, and re-layouts: 10.3 us -> 5.2 us
  Pallas kernels: 126 us -> 131 us
  other arithmetic: 2.81 us -> 0 us
    pallas_call x2, Pallas kernels: 126 us -> 131 us  [the longest x1 125 us: contract(): pl.pallas_call(functools.partial(contract_kernel, workers), out_shape=jax...]
    select_n x3 -> x0, other arithmetic: 1.99 us -> none  [the longest x2 1.91 us: per_device(): w = jnp.where(slots < own_count, weights[own_ids], 0.0)]
    dynamic_slice x2 -> x0, local copies, waits for them, and re-layouts: 1.94 us -> none  [the longest x1 1.36 us: per_device(): own_count = lax.dynamic_index_in_dim(sink_counts, own, 0, keepdims=False)]
    gather x2 -> x0, local copies, waits for them, and re-layouts: 1.92 us -> none  [the longest x1 1.3 us: per_device(): w = jnp.where(slots < own_count, weights[own_ids], 0.0)]
    unnamed x5 -> x2, local copies, waits for them, and re-layouts: 5.44 us -> 4.51 us
where the time goes in v1:
time: 137 us
  Pallas kernels  131 us (96%)
  local copies, waits for them, and re-layouts  5.2 us (4%)
    pallas_call x1, Pallas kernels, contract(): pl.pallas_call(functools.partial(contract_kernel, workers), out_shape=jax...  125 us
    pallas_call x1, Pallas kernels, pick(): pl.pallas_call(pick_kernel, out_shape=(jax.ShapeDtypeStruct((sinks,) + so...  6.1 us
    unnamed x2, local copies, waits for them, and re-layouts  4.51 us

profile of v1, /device:TPU:29, one launch (start us, length us, event | category | flops | bytes accessed | tf_op | source)
XLA Modules:
  0.0 136.5 jit_solution(3768928599786933832)
XLA Ops:
  0.0 0.8 copy.8
  0.8 0.7 reshape.9.legs_ids_ref
  1.5 6.1 %pick.1 = (bf16[16,8,128,128]{3,2,1,0:T(8,128)(2,1)}, bf16[16,18,8,128]{3,2,1,0:T(8,128)(2,1)}) custom-call(s32[16]{0:T(128)} %ids_ref.1, s32[144]{0:T(256)} %reshape.9.legs_ids_ref, s32[16]{0:T(128)} %counts_ref.3, bf16[16,8,128,128]{3,2,1,0:T(8,128)(2,1)} %bitcast.3, bf16[96,1024]{1,0:T(8,128)(2,1)} %p_ref.1), custom_call_target="tpu_custom_call" | custom-call | tf_op jit(solution)/shard_map/pick/pallas_call | solution.py:55
  7.6 125.2 %contract.1 = bf16[128,128,128]{2,1,0:T(8,128)(2,1)} custom-call(s32[16]{0:T(128)} %counts_ref.3, f32[48]{0:T(128)} %weights_ref.1, s32[5,1,192]{2,1,0:T(1,128)} %constant.2.clone.key_ref, bf16[16,8,128,128]{3,2,1,0:T(8,128)(2,1)} %get-tuple-element.7.x_ref, bf16[16,18,8,128]{3,2,1,0:T(8,128)(2,1)} %get-tuple-element.8.legs_ref), custom_call_target="tpu_custom_call" | custom-call | tf_op jit(solution)/shard_map/contract/pallas_call | solution.py:294
  132.8 3.7 %copy.10 = bf16[1,16384,128]{2,1,0:T(8,128)(2,1)} copy(bf16[1,16384,128]{2,1,0:T(8,128)(2,1)} %bitcast.2) | data formatting | bytes 8388608

commit v2 on v1

--- a/solution.py
+++ b/solution.py
@@ -15,28 +15,24 @@
 
 
 def pick_kernel(
-    ids_ref, legs_ids_ref, counts_ref, x_ref, p_ref, o_ref, l_ref, buf, rows, in_sem, out_sem
+    ids_ref, legs_ids_ref, counts_ref, x_ref, p_ref, o_ref, l_ref, rows, sem
 ):
     sinks = o_ref.shape[0]
-    diagrams = legs_ids_ref.shape[0] // LEGS
+    diagrams = legs_ids_ref.shape[1]
     own_rows, extent = l_ref.shape[2], l_ref.shape[3]
-    load = pltpu.make_async_copy(x_ref, buf, in_sem)
-    load.start()
+
+    @pl.loop(0, sinks)
+    def _(s):
+        pltpu.make_async_copy(x_ref.at[ids_ref[s]], o_ref.at[s], sem.at[s]).start()
 
     for r in range(own_rows):
         rows[:, r, :] = p_ref[:, r * extent : (r + 1) * extent].astype(jnp.float32)
-
-    load.wait()
-
-    @pl.loop(0, sinks)
-    def _(s):
-        pltpu.make_async_copy(buf.at[ids_ref[s]], o_ref.at[s], out_sem.at[s]).start()
 
     def one(s, start):
         for slot in range(MOST):
             d = jnp.minimum(start + slot, diagrams - 1)
             for leg in range(LEGS):
-                l_ref[s, slot * LEGS + leg] = rows[legs_ids_ref[d * LEGS + leg]].astype(
+                l_ref[s, slot * LEGS + leg] = rows[legs_ids_ref[leg, d]].astype(
                     jnp.bfloat16
                 )
         return start + counts_ref[s]
@@ -45,7 +41,7 @@
 
     @pl.loop(0, sinks)
     def _(s):
-        pltpu.make_async_copy(buf.at[0], o_ref.at[s], out_sem.at[s]).wait()
+        pltpu.make_async_copy(x_ref.at[0], o_ref.at[s], sem.at[s]).wait()
 
 
 def pick(sources, perambs, source_ids, leg_ids, counts):
@@ -66,16 +62,14 @@
             pl.BlockSpec(memory_space=pltpu.VMEM),
         ],
         out_specs=(
-            pl.BlockSpec(memory_space=pl.ANY),
+            pl.BlockSpec(memory_space=pltpu.VMEM),
             pl.BlockSpec(memory_space=pltpu.VMEM),
         ),
         scratch_shapes=[
-            pltpu.VMEM(sources.shape, sources.dtype),
             pltpu.VMEM((perambs.shape[0], own_rows, extent), jnp.float32),
-            pltpu.SemaphoreType.DMA,
             pltpu.SemaphoreType.DMA((sinks,)),
         ],
-        compiler_params=pltpu.CompilerParams(vmem_limit_bytes=60 * 1024 * 1024),
+        compiler_params=pltpu.CompilerParams(vmem_limit_bytes=12 * 1024 * 1024),
         name="pick",
     )(source_ids, leg_ids, counts, sources, perambs)
 
@@ -105,13 +99,11 @@
     mid,
     acc,
     stage,
-    obuf,
     own_sem,
     xsend,
     xrecv,
     lsend,
     lrecv,
-    out_sem,
 ):
     own_a, extent = xbuf.shape[0], xbuf.shape[2]
     diagrams = weights_ref.shape[0]
@@ -266,13 +258,7 @@
                     for h, (at, piece) in enumerate(pieces(2 * b + half)):
                         stage[:, half * wide + h, :] = piece
                 at = pl.ds(pl.multiple_of(2 * wide * b, 2 * wide), 2 * wide)
-                obuf[:, at, :] = stage[:, : 2 * wide, :].astype(jnp.bfloat16)
-                pltpu.make_async_copy(obuf.at[:, at], o_ref.at[:, at], out_sem.at[b]).start()
-
-            @pl.loop(0, extent // (2 * wide))
-            def _(b):
-                at = pl.ds(pl.multiple_of(2 * wide * b, 2 * wide), 2 * wide)
-                pltpu.make_async_copy(obuf.at[:, at], o_ref.at[:, at], out_sem.at[b]).wait()
+                o_ref[:, at, :] = stage[:, : 2 * wide, :].astype(jnp.bfloat16)
 
 
 def contract(x, legs, counts, weights, workers):
@@ -301,7 +287,7 @@
             pl.BlockSpec(memory_space=pl.ANY),
             pl.BlockSpec(memory_space=pl.ANY),
         ],
-        out_specs=pl.BlockSpec(memory_space=pl.ANY),
+        out_specs=pl.BlockSpec(memory_space=pltpu.VMEM),
         scratch_shapes=[
             pltpu.VMEM((own_a, workers, extent, extent), jnp.bfloat16),
             pltpu.VMEM((workers,) + legs.shape[1:], jnp.bfloat16),
@@ -312,16 +298,14 @@
             pltpu.VMEM((MOST * most * step, extent), jnp.float32),
             pltpu.VMEM((extent * extent, extent), jnp.float32),
             pltpu.VMEM((extent, 24, extent), jnp.float32),
-            pltpu.VMEM((extent, extent, extent), jnp.bfloat16),
             pltpu.SemaphoreType.DMA((own_a + 1,)),
             pltpu.SemaphoreType.DMA((own_a, workers)),
             pltpu.SemaphoreType.DMA((own_a, workers)),
             pltpu.SemaphoreType.DMA((workers,)),
             pltpu.SemaphoreType.DMA((workers,)),
-            pltpu.SemaphoreType.DMA((extent // 16,)),
         ],
         compiler_params=pltpu.CompilerParams(
-            vmem_limit_bytes=62 * 1024 * 1024, collective_id=0, has_side_effects=True
+            vmem_limit_bytes=MOST * most * step * extent * 4 + 26 * 1024 * 1024, collective_id=0, has_side_effects=True
         ),
         name="contract",
     )(counts, weights, jnp.asarray(keys, jnp.int32), x, legs)
@@ -335,7 +319,7 @@
         sources.reshape(-1, own_a, extent, extent),
         perambs,
         source_ids,
-        peramb_ids.reshape(-1),
+        peramb_ids.T,
         sink_counts,
     )
     total = contract(picked, legs, sink_counts, weights, workers)

time: 137 us -> 134 us (0.978)
  Pallas kernels: 131 us -> 126 us
  local copies, waits for them, and re-layouts: 5.2 us -> 7.16 us
    pallas_call x1, Pallas kernels: 6.1 us -> 2.06 us  [pick(): pl.pallas_call(pick_kernel, out_shape=(jax.ShapeDtypeStruct((sinks,) + so...]
    unnamed x2 -> x17, local copies, waits for them, and re-layouts: 4.51 us -> 7.16 us
where the time goes in v2:
time: 134 us
  Pallas kernels  126 us (94%)
  local copies, waits for them, and re-layouts  7.16 us (5%)
    pallas_call x1, Pallas kernels, contract(): pl.pallas_call(functools.partial(contract_kernel, workers), out_shape=jax...  124 us
    unnamed x17, local copies, waits for them, and re-layouts  7.16 us

profile of v2, /device:TPU:29, one launch (start us, length us, event | category | flops | bytes accessed | tf_op | source)
XLA Modules:
  0.0 133.5 jit_solution(17629030763999030048)
XLA Ops:
  0.0 0.0 copy-start.5
  0.0 0.0 copy-start.7
  0.0 0.0 copy-start
  0.0 2.2 %copy-done = bf16[16,1024,128]{2,1,0:T(8,128)(2,1)S(1)} copy-done((bf16[16,1024,128]{2,1,0:T(8,128)(2,1)S(1)}, bf16[16,1024,128]{2,1,0:T(8,128)(2,1)}, u32[]{:S(2)}) %copy-start) | copy-done | bytes 4194328
  2.2 0.0 copy-start.1
  2.2 0.9 copy-done.1
  3.1 0.0 copy-start.3
  3.1 0.7 copy-done.3
  3.8 0.0 copy-start.4
  3.8 0.7 copy-done.4
  4.5 0.0 copy-start.6
  4.5 0.7 copy-done.6
  5.1 0.0 copy-start.2
  5.1 2.1 %pick.1 = (bf16[16,8,128,128]{3,2,1,0:T(8,128)(2,1)S(1)}, bf16[16,18,8,128]{3,2,1,0:T(8,128)(2,1)S(1)}) custom-call(s32[16]{0:T(128)S(1)} %copy-done.6, s32[3,48]{1,0:T(4,128)S(1)} %bitcast.5, s32[16]{0:T(128)S(1)} %copy-done.4, bf16[16,8,128,128]{3,2,1,0:T(8,128)(2,1)S(1)} %bitcast.4, bf16[96,1024]{1,0:T(8,128)(2,1)S(1)} %copy-done.1), custom_call_target="tpu_custom_call" | custom-call | tf_op jit(solution)/shard_map/pick/pallas_call | solution.py:51
  7.2 0.0 copy-done.5
  7.2 0.0 copy-done.7
  7.2 0.0 copy-done.2
  7.2 124.3 %contract.1 = bf16[128,128,128]{2,1,0:T(8,128)(2,1)S(1)} custom-call(s32[16]{0:T(128)S(1)} %copy-done.5, f32[48]{0:T(128)S(1)} %copy-done.7, s32[5,1,192]{2,1,0:T(1,128)S(1)} %copy-done.2, bf16[16,8,128,128]{3,2,1,0:T(8,128)(2,1)S(1)} %get-tuple-element.7.x_ref, bf16[16,18,8,128]{3,2,1,0:T(8,128)(2,1)S(1)} %get-tuple-element.8.legs_ref), custom_call_target="tpu_custom_call" | custom-call | tf_op jit(solution)/shard_map/contract/pallas_call | solution.py:280
  131.5 2.0 %copy.9 = bf16[1,16384,128]{2,1,0:T(8,128)(2,1)} copy(bf16[1,16384,128]{2,1,0:T(8,128)(2,1)S(1)} %bitcast.3) | data formatting | bytes 8388608
Async XLA Ops:
  0.0 7.2 %copy-start.5 = (s32[16]{0:T(128)S(1)}, s32[16]{0:T(128)}, u32[]{:S(2)}) copy-start(s32[16]{0:T(128)} %counts_ref.3) | copy-start | bytes 196
  0.0 7.2 %copy-start.7 = (f32[48]{0:T(128)S(1)}, f32[48]{0:T(128)}, u32[]{:S(2)}) copy-start(f32[48]{0:T(128)} %weights_ref.1) | copy-start | bytes 580
  0.0 2.2 %copy-start = (bf16[16,1024,128]{2,1,0:T(8,128)(2,1)S(1)}, bf16[16,1024,128]{2,1,0:T(8,128)(2,1)}, u32[]{:S(2)}) copy-start(bf16[16,1024,128]{2,1,0:T(8,128)(2,1)} %param.7) | copy-start | bytes 12582916
  2.2 0.9 copy-start.1
  3.1 0.7 copy-start.3
  3.8 0.7 copy-start.4
  4.5 0.7 copy-start.6
  5.1 2.1 %copy-start.2 = (s32[5,1,192]{2,1,0:T(1,128)S(1)}, s32[5,1,192]{2,1,0:T(1,128)}, u32[]{:S(2)}) copy-start(s32[5,1,192]{2,1,0:T(1,128)} %constant.2.clone.key_ref) | copy-start | bytes 11524
